TPU v7x, 32 devices: a whole 2x2x4 slice. The times are simulated.
32 devices in a mesh: fsdp: 8 (over y, x, core), tp: 4 (over z).
Axes of the slice: x: 2, y: 2, z: 4, core: 2. Of those that a mesh axis runs over, the one named last changes fastest.
Arguments:
- layer_input: bfloat16 [8192, 2048], P(('fsdp', 'tp')), may hold values from -6 to 6
- teacher: bfloat16 [8192, 2048], P(('fsdp', 'tp')), may hold values from -6 to 6
- out_grad: bfloat16 [8192, 2048], P(('fsdp', 'tp')), may hold values from -6 to 6
- lengths: int32 [8], P('fsdp'), may hold values from 512 to 1024, as said below
- norm_gain: float32 [2048], P(('fsdp', 'tp')), may hold values from 0.5 to 1.5
- norm_bias: float32 [2048], P(('fsdp', 'tp')), may hold values from -4 to 4
- qkv_weight: bfloat16 [3, 2048, 2048], P(None, 'fsdp', 'tp'), may hold values from -0.125 to 0.125
- qkv_bias: bfloat16 [3, 2048], P(None, ('tp', 'fsdp')), may hold values from -4 to 4
- out_weight: bfloat16 [2048, 2048], P('tp', 'fsdp'), may hold values from -1 to 1
- gate_up_weight: bfloat16 [2, 2048, 5632], P(None, 'fsdp', 'tp'), may hold values from -0.125 to 0.125
- down_weight: bfloat16 [5632, 2048], P('tp', 'fsdp'), may hold values from -0.078125 to 0.078125
Outputs:
- output: bfloat16 [8192, 2048], P(('fsdp', 'tp'))
- loss: float32 [], replicated
- input_grad: bfloat16 [8192, 2048], P(('fsdp', 'tp'))
- norm_gain_grad: float32 [2048], P(('fsdp', 'tp'))
- norm_bias_grad: float32 [2048], P(('fsdp', 'tp'))
- qkv_weight_grad: float32 [3, 2048, 2048], P(None, 'fsdp', 'tp')
- qkv_bias_grad: float32 [3, 2048], P(None, ('tp', 'fsdp'))
- out_weight_grad: float32 [2048, 2048], P('tp', 'fsdp')
- gate_up_weight_grad: float32 [2, 2048, 5632], P(None, 'fsdp', 'tp')
- down_weight_grad: float32 [5632, 2048], P('tp', 'fsdp')
Inputs may be any that keep to these rules, and one draw needn't show every extreme that they name: `lengths`: each slot holds at least half of its 1024 positions; some slot is full in every draw.
All inputs are finite; a program needn't handle non-finite values.
Results may differ from a plain program's by a relative error of at most 0.0084.
Values may be sent and summed in bfloat16 or wider, within the bound.
No kernel may reach another device: no remote copies, remote signals or barrier semaphores. Data moves between devices by JAX's collectives and lax.ppermute only.
A program may use at most 256 MiB of HBM per device.

v0:
```python
import jax
import jax.numpy as jnp
from jax import lax
from jax.sharding import PartitionSpec as P

D = 2048
HD = 64
ROT = 16
SEQ = 1024
SEQS_DEV = 1
epsilon = 1e-05


def rotary_tables(row_total):
    half_rot = ROT // 2
    positions = (jnp.arange(row_total, dtype=jnp.int32) % SEQ).astype(jnp.float32)
    frequency = 10000.0 ** (-2.0 * jnp.arange(half_rot, dtype=jnp.float32) / ROT)
    angles = positions[:, None] * frequency[None, :]
    angles = jnp.concatenate([angles, angles], -1)[:, None, :]
    return (jnp.cos(angles), jnp.sin(angles))


def turn_heads(vectors, cos_tab, sine_tab):
    half_rot = ROT // 2
    head_part = vectors[..., :ROT]
    turned = jnp.concatenate([-head_part[..., half_rot:], head_part[..., :half_rot]], -1)
    return jnp.concatenate([head_part * cos_tab + turned * sine_tab, vectors[..., ROT:]], -1)


def unturn_heads(vectors, cos_tab, sine_tab):
    half_rot = ROT // 2
    head_part = vectors[..., :ROT]
    by_sine = head_part * sine_tab
    back_part = jnp.concatenate([by_sine[..., half_rot:], -by_sine[..., :half_rot]], -1)
    return jnp.concatenate([head_part * cos_tab + back_part, vectors[..., ROT:]], -1)


def per_device(
    layer_input,
    teacher,
    out_grad,
    lengths,
    norm_gain,
    norm_bias,
    qkv_weight,
    qkv_bias,
    out_weight,
    gate_up_weight,
    down_weight,
):
    local_rows = layer_input.shape[0]
    group_rows = SEQS_DEV * SEQ
    gain_vec, shift_vec = (
        lax.all_gather(norm_gain, ("fsdp", "tp"), axis=0, tiled=True),
        lax.all_gather(norm_bias, ("fsdp", "tp"), axis=0, tiled=True),
    )
    w_qkv, b_qkv, w_out, w_gu, w_down = (
        lax.all_gather(qkv_weight, "fsdp", axis=1, tiled=True),
        lax.all_gather(qkv_bias, "fsdp", axis=1, tiled=True),
        lax.all_gather(out_weight, "fsdp", axis=1, tiled=True),
        lax.all_gather(gate_up_weight, "fsdp", axis=1, tiled=True),
        lax.all_gather(down_weight, "fsdp", axis=1, tiled=True),
    )
    row_ids = lax.axis_index("tp") * local_rows + jnp.arange(local_rows, dtype=jnp.int32)
    row_pick = (row_ids // SEQ)[:, None] == jnp.arange(SEQS_DEV, dtype=jnp.int32)[None, :]
    row_length = jnp.sum(jnp.where(row_pick, lengths[None, :], 0), 1)
    valid_rows = (row_ids % SEQ < row_length).astype(jnp.float32)
    inputs = layer_input.astype(jnp.float32)
    center = inputs - jnp.mean(inputs, -1, keepdims=True)
    inv_std = lax.rsqrt(jnp.mean(center * center, -1, keepdims=True) + epsilon)
    unit_rows = center * inv_std
    normed = (unit_rows * gain_vec + shift_vec).astype(jnp.bfloat16)
    all_normed = lax.all_gather(normed, "tp", axis=0, tiled=True)
    local_width = w_qkv.shape[2]
    local_heads = local_width // HD
    cos_tab, sine_tab = rotary_tables(group_rows)
    joined_qkv = jnp.einsum(
        "sd,jde->jse", all_normed, w_qkv, preferred_element_type=jnp.float32
    ) + b_qkv[:, None, :].astype(jnp.float32)
    queries = turn_heads(
        joined_qkv[0].reshape(group_rows, local_heads, HD), cos_tab, sine_tab
    ).astype(jnp.bfloat16)
    key_rows = turn_heads(
        joined_qkv[1].reshape(group_rows, local_heads, HD), cos_tab, sine_tab
    ).astype(jnp.bfloat16)
    values = joined_qkv[2].reshape(group_rows, local_heads, HD).astype(jnp.bfloat16)
    span_rows = min(512, SEQ)
    score_scale = HD ** (-0.5)
    key_pos = jnp.arange(SEQ, dtype=jnp.int32)
    block_count = group_rows // span_rows
    block_ids = jnp.arange(block_count, dtype=jnp.int32)

    def block_scores(block_id):
        row_start = block_id * span_rows
        seq_start = row_start // SEQ * SEQ
        q_block = lax.dynamic_slice_in_dim(queries, row_start, span_rows, 0)
        scores = (
            jnp.einsum("qhe,khe->hqk", q_block, key_rows, preferred_element_type=jnp.float32)
            * score_scale
        )
        query_pos = row_start - seq_start + jnp.arange(span_rows, dtype=jnp.int32)
        allowed = (key_pos[None, :] <= query_pos[:, None])[None]
        scores = jnp.where(allowed, scores, -1e30)
        return (row_start, seq_start, q_block, key_rows, values, scores, allowed)

    def attend(block_id):
        row_start, seq_start, q_block, k_seq, v_seq, scores, allowed = block_scores(block_id)
        row_max = jnp.max(scores, -1, keepdims=True)
        shifted = jnp.exp(scores - row_max)
        totals = jnp.sum(shifted, -1, keepdims=True)
        weights = (shifted / totals).astype(jnp.bfloat16)
        out_block = jnp.einsum("hqk,khe->qhe", weights, v_seq, preferred_element_type=jnp.float32)
        return (out_block, row_max + jnp.log(totals))

    attended, log_sums = lax.map(attend, block_ids)
    attn_rows = attended.reshape(group_rows, local_width).astype(jnp.bfloat16)
    gate_up = jnp.einsum("sd,jdf->jsf", all_normed, w_gu, preferred_element_type=jnp.float32)
    sigmoid_gate = jax.nn.sigmoid(gate_up[0])
    hidden = (gate_up[0] * sigmoid_gate * gate_up[1]).astype(jnp.bfloat16)
    branch_sum = lax.psum_scatter(
        jnp.dot(attn_rows, w_out, preferred_element_type=jnp.float32)
        + jnp.dot(hidden, w_down, preferred_element_type=jnp.float32),
        "tp",
        scatter_dimension=0,
        tiled=True,
    )
    result = inputs + valid_rows[:, None] * branch_sum
    mismatch = result - teacher.astype(jnp.float32)
    loss_part = jnp.sum(valid_rows[:, None] * mismatch * mismatch)
    count_part = jnp.sum(valid_rows)
    loss_total, valid_total = lax.psum((loss_part, count_part), ("fsdp", "tp"))
    loss_value = loss_total / (valid_total * D)
    seed_rows = valid_rows[:, None] * (out_grad.astype(jnp.float32) + mismatch)
    all_seed = lax.all_gather(seed_rows.astype(jnp.bfloat16), "tp", axis=0, tiled=True)
    w_qkv, w_out, w_gu, w_down = (
        lax.all_gather(qkv_weight, "fsdp", axis=1, tiled=True),
        lax.all_gather(out_weight, "fsdp", axis=1, tiled=True),
        lax.all_gather(gate_up_weight, "fsdp", axis=1, tiled=True),
        lax.all_gather(down_weight, "fsdp", axis=1, tiled=True),
    )
    grad_out_w = jnp.einsum("sa,sd->ad", attn_rows, all_seed, preferred_element_type=jnp.float32)
    grad_attn = (
        jnp.einsum("sd,ad->sa", all_seed, w_out, preferred_element_type=jnp.float32)
        .astype(jnp.bfloat16)
        .reshape(group_rows, local_heads, HD)
    )
    grad_down = jnp.einsum("sf,sd->fd", hidden, all_seed, preferred_element_type=jnp.float32)
    grad_hidden = jnp.einsum("sd,fd->sf", all_seed, w_down, preferred_element_type=jnp.float32)
    grad_gate = grad_hidden * gate_up[1] * sigmoid_gate * (1.0 + gate_up[0] * (1.0 - sigmoid_gate))
    grad_up = grad_hidden * gate_up[0] * sigmoid_gate
    grad_gu = jnp.stack([grad_gate, grad_up]).astype(jnp.bfloat16)
    grad_gu_w = jnp.einsum("sd,jsf->jdf", all_normed, grad_gu, preferred_element_type=jnp.float32)

    def attend_back(kv_grads, block_id):
        grad_keys, grad_values = kv_grads
        row_start, seq_start, q_block, k_seq, v_seq, scores, allowed = block_scores(block_id)
        probs = jnp.where(allowed, jnp.exp(scores - log_sums[block_id]), 0.0)
        d_block = lax.dynamic_slice_in_dim(grad_attn, row_start, span_rows, 0)
        grad_probs = jnp.einsum("qhe,khe->hqk", d_block, v_seq, preferred_element_type=jnp.float32)
        inner = jnp.sum(probs * grad_probs, -1, keepdims=True)
        grad_scores = (probs * (grad_probs - inner)).astype(jnp.bfloat16)
        grad_query = (
            jnp.einsum("hqk,khe->qhe", grad_scores, k_seq, preferred_element_type=jnp.float32)
            * score_scale
        )
        key_part = (
            jnp.einsum("hqk,qhe->khe", grad_scores, q_block, preferred_element_type=jnp.float32)
            * score_scale
        )
        value_part = jnp.einsum(
            "hqk,qhe->khe", probs.astype(jnp.bfloat16), d_block, preferred_element_type=jnp.float32
        )
        key_now = grad_keys
        grad_keys = key_now + key_part
        value_now = grad_values
        grad_values = value_now + value_part
        return ((grad_keys, grad_values), grad_query)

    zero_heads = jnp.zeros((group_rows, local_heads, HD), jnp.float32)
    (grad_keys, grad_values), grad_queries = lax.scan(
        attend_back, (zero_heads, zero_heads), block_ids
    )
    grad_queries = grad_queries.reshape(group_rows, local_heads, HD)
    grad_qkv = (
        jnp.stack(
            [
                unturn_heads(grad_queries, cos_tab, sine_tab),
                unturn_heads(grad_keys, cos_tab, sine_tab),
                grad_values,
            ]
        )
        .reshape(3, group_rows, local_width)
        .astype(jnp.bfloat16)
    )
    grad_bias = jnp.sum(grad_qkv, 1, dtype=jnp.float32)
    grad_qkv_w = jnp.einsum("sd,jse->jde", all_normed, grad_qkv, preferred_element_type=jnp.float32)
    grad_normed = lax.psum_scatter(
        jnp.einsum("jse,jde->sd", grad_qkv, w_qkv, preferred_element_type=jnp.float32)
        + jnp.einsum("jsf,jdf->sd", grad_gu, w_gu, preferred_element_type=jnp.float32),
        "tp",
        scatter_dimension=0,
        tiled=True,
    )
    gain_grad_part = jnp.sum(grad_normed * unit_rows, 0)
    bias_grad_part = jnp.sum(grad_normed, 0)
    grad_unit = grad_normed * gain_vec
    grad_inputs = inv_std * (
        grad_unit
        - jnp.mean(grad_unit, -1, keepdims=True)
        - unit_rows * jnp.mean(grad_unit * unit_rows, -1, keepdims=True)
    )
    input_grad = (seed_rows + grad_inputs).astype(jnp.bfloat16)
    gain_grad, bias_grad = (
        lax.psum_scatter(gain_grad_part, ("fsdp", "tp"), scatter_dimension=0, tiled=True),
        lax.psum_scatter(bias_grad_part, ("fsdp", "tp"), scatter_dimension=0, tiled=True),
    )
    qkv_w_grad, qkv_b_grad, out_w_grad, gu_w_grad, down_w_grad = (
        lax.psum_scatter(grad_qkv_w, "fsdp", scatter_dimension=1, tiled=True),
        lax.psum_scatter(grad_bias, "fsdp", scatter_dimension=1, tiled=True),
        lax.psum_scatter(grad_out_w, "fsdp", scatter_dimension=1, tiled=True),
        lax.psum_scatter(grad_gu_w, "fsdp", scatter_dimension=1, tiled=True),
        lax.psum_scatter(grad_down, "fsdp", scatter_dimension=1, tiled=True),
    )
    return (
        result.astype(jnp.bfloat16),
        loss_value,
        input_grad,
        gain_grad,
        bias_grad,
        qkv_w_grad,
        qkv_b_grad,
        out_w_grad,
        gu_w_grad,
        down_w_grad,
    )


def solution(mesh):
    placed = (
        P(("fsdp", "tp"), None),
        P(("fsdp", "tp"), None),
        P(("fsdp", "tp"), None),
        P("fsdp"),
        P(("fsdp", "tp")),
        P(("fsdp", "tp")),
        P(None, "fsdp", "tp"),
        P(None, ("tp", "fsdp")),
        P("tp", "fsdp"),
        P(None, "fsdp", "tp"),
        P("tp", "fsdp"),
    )
    return jax.shard_map(
        per_device,
        mesh=mesh,
        in_specs=placed,
        out_specs=(
            P(("fsdp", "tp"), None),
            P(),
            P(("fsdp", "tp"), None),
            P(("fsdp", "tp")),
            P(("fsdp", "tp")),
            P(None, "fsdp", "tp"),
            P(None, ("tp", "fsdp")),
            P("tp", "fsdp"),
            P(None, "fsdp", "tp"),
            P("tp", "fsdp"),
        ),
        check_vma=False,
    )
```

profile of v0, /device:TPU:0, one launch (start us, length us, event | category | flops | bytes accessed | tf_op | source)
XLA Modules:
  0.0 1318.2 jit_solution(7497582739152333700)
XLA Ops:
  12.2 42.0 %all-reduce.5 = (f32[2048]{0:T(1024)S(1)}, f32[2048]{0:T(1024)S(1)}) all-reduce(f32[2048]{0:T(1024)S(1)} %dynamic-update-slice.1, f32[2048]{0:T(1024)S(1)} %dynamic-update-slice), channel_id=1, replica_groups=mesh['fsdp'=8,'tp'=4] {'fsdp','tp'}, use_global_device_ids=true, to_apply=%add.1 | all-reduce | flops 4096 | bytes 32768
  54.2 2.7 fusion.44
  60.2 10.2 all-gather
  70.7 67.1 %all-gather.8.cloned.1.call-done = bf16[1024,2048]{1,0:T(8,128)(2,1)} async-done(((bf16[256,2048]{1,0:T(8,128)(2,1)}), bf16[1024,2048]{1,0:T(8,128)(2,1)}) %all-gather.8.cloned.1.call-update) | async-done | bytes 4194320 | tf_op jit(solution)/shard_map/all_gather | solution.py:73
  137.8 47.7 %all-gather.10.cloned.1.call-done = bf16[3,2048,512]{1,2,0:T(8,128)(2,1)} async-done(((bf16[3,256,512]{1,2,0:T(8,128)(2,1)}), bf16[3,2048,512]{1,2,0:T(8,128)(2,1)}) %all-gather.10.cloned.1.call-update) | async-done | bytes 6291472 | tf_op jit(solution)/shard_map/all_gather | solution.py:58
  185.4 10.1 add_bitcast_fusion
  199.0 32.1 %while.32 = (s32[]{:T(128)}, bf16[2,512,8,64]{1,3,2,0:T(8,128)(2,1)S(1)}, f32[2,8,512,1]{2,1,3,0:T(8,128)S(1)}, s32[2]{0:T(128)S(1)}, bf16[1024,8,64]{0,2,1:T(8,...) while((s32[]{:T(128)}, ...), condition=%wide.region_5.6_spmd.clone, body=%wide.region_2.5_spmd.clone.sunk | while | flops 1124594176 | bytes 56234364 | solution.py:115
  200.6 4.1 fusion.118
  204.8 4.2 fusion.119
  209.0 5.9 fusion.120
  216.6 4.1 fusion.118
  220.7 4.2 fusion.119
  225.0 5.9 fusion.120
  232.5 22.6 %all-gather.14.cloned.1.call-done = bf16[2,2048,1408]{2,1,0:T(8,128)(2,1)} async-done(((bf16[2,256,1408]{2,1,0:T(8,128)(2,1)}), bf16[2,2048,1408]{2,1,0:T(8,128)(2,1)}) %all-gather.14.cloned.1.call-update) | async-done | bytes 11534352 | tf_op jit(solution)/shard_map/all_gather | solution.py:61
  255.1 17.2 %convolution_bitcast_fusion.1 = f32[2,1024,1408]{2,1,0:T(8,128)S(1)} fusion(bf16[2,2048,1408]{2,1,0:T(8,128)(2,1)} %all-gather.14.cloned.1.call-done, bf16[1024,2048]{1,0:T(8,128)(2,1)} %all-gather.8.cloned.1.call-done), kind=kOutput, calls=%fused_computation.41 | convolution fusion | flops 11811160064 | bytes 27262976 | tf_op jit(solution)/shard_map/sd,jdf->jsf/dot_general | solution.py:117
  272.3 4.2 copy-done.8
  276.5 2.8 multiply_convert_fusion.3
  279.3 21.9 %all-gather.16.cloned.1.call-done = bf16[1408,2048]{1,0:T(8,128)(2,1)} async-done(((bf16[1408,256]{1,0:T(8,128)(2,1)}), bf16[1408,2048]{1,0:T(8,128)(2,1)}) %all-gather.16.cloned.1.call-update) | async-done | bytes 5767184 | tf_op jit(solution)/shard_map/all_gather | solution.py:62
  301.2 11.6 fusion.74
  312.8 18.3 %all-gather.12.cloned.1.call-done = bf16[512,2048]{1,0:T(8,128)(2,1)} async-done(((bf16[512,256]{1,0:T(8,128)(2,1)}), bf16[512,2048]{1,0:T(8,128)(2,1)}) %all-gather.12.cloned.1.call-update) | async-done | bytes 2097168 | tf_op jit(solution)/shard_map/all_gather | solution.py:60
  331.2 9.7 convolution_add_fusion
  341.7 143.8 %reduce-scatter.10.cloned.1.call-done = f32[256,2048]{1,0:T(8,128)} async-done(((f32[1024,2048]{1,0:T(8,128)}), f32[256,2048]{1,0:T(8,128)}) %reduce-scatter.10.cloned.1.call-update) | async-done | bytes 2097168 | tf_op jit(solution)/shard_map/reduce_scatter | solution.py:120
  485.5 3.7 fusion.59
  489.3 81.6 %all-gather.18.cloned.1.call-done = bf16[1024,2048]{1,0:T(8,128)(2,1)} async-done(((bf16[256,2048]{1,0:T(8,128)(2,1)}), bf16[1024,2048]{1,0:T(8,128)(2,1)}) %all-gather.18.cloned.1.call-update) | async-done | bytes 4194320 | tf_op jit(solution)/shard_map/all_gather | solution.py:134
  570.8 6.2 convolution_convert_fusion
  577.1 134.3 %while.33 = (s32[]{:T(128)}, f32[1024,8,64]{0,2,1:T(8,128)}, f32[1024,8,64]{0,2,1:T(8,128)}, f32[2,512,8,64]{1,0,3,2:T(2,128)}, s32[2]{0:T(128)S(1)}, /*index=5*...) while((s32[]{:T(128)}, f32[1024,8,64]{0,2,1:T(8,128)}, ...), condition=%wide.region_13.14_spmd.clone, body=%wide.region_11.13_spmd.clone.sunk | while | flops 2729701888 | bytes 200626816 | solution.py:180
  582.4 3.8 fusion.130
  586.2 12.2 multiply_reduce_fusion.3
  598.4 9.4 multiply_convert_fusion.5
  607.8 8.9 bitcast_add_fusion.6
  616.7 2.7 fusion.131
  619.4 2.9 bitcast_add_fusion.5
  622.3 2.0 copy.85
  624.3 19.7 %dynamic_update_slice.30 = f32[2,512,8,64]{1,0,3,2:T(2,128)} dynamic-update-slice(f32[2,512,8,64]{1,0,3,2:T(2,128)} %get-tuple-element.597, f32[1,512,8,64]{1,0,3,2:T(1,128)} %copy.85, s32[]{:T(128)S(6)} %copy.104, s32[]{:T(128)} %constant.200.clone.1..sunk.1, s32[]{:T(128)} %constant.200.clone.1..sunk.1, s32[]{:T(128)} %constant.200.clone.1..sunk.1) | dynamic-update-slice | bytes 2097156 | tf_op jit(solution)/shard_map/while/body/jit(dynamic_update_index_in_dim)/dynamic_update_slice | solution.py:115
  649.0 3.8 fusion.130
  652.8 12.3 multiply_reduce_fusion.3
  665.0 9.4 multiply_convert_fusion.5
  674.4 9.5 bitcast_add_fusion.6
  684.0 2.7 fusion.131
  686.6 2.9 bitcast_add_fusion.5
  689.5 2.0 copy.85
  691.6 19.7 %dynamic_update_slice.30 = f32[2,512,8,64]{1,0,3,2:T(2,128)} dynamic-update-slice(f32[2,512,8,64]{1,0,3,2:T(2,128)} %get-tuple-element.597, f32[1,512,8,64]{1,0,3,2:T(1,128)} %copy.85, s32[]{:T(128)S(6)} %copy.104, s32[]{:T(128)} %constant.200.clone.1..sunk.1, s32[]{:T(128)} %constant.200.clone.1..sunk.1, s32[]{:T(128)} %constant.200.clone.1..sunk.1) | dynamic-update-slice | bytes 2097156 | tf_op jit(solution)/shard_map/while/body/jit(dynamic_update_index_in_dim)/dynamic_update_slice | solution.py:115
  711.4 4.2 reshape.270
  721.2 2.7 convert.56
  726.8 15.7 %fusion.34 = (bf16[1,1024,1408]{2,1,0:T(8,128)(2,1)}, bf16[1,1024,1408]{2,1,0:T(8,128)(2,1)}) fusion(f32[2,1024,1408]{2,1,0:T(8,128)} %copy-done.8, bf16[1024,2048]{1,0:T(8,128)(2,1)} %all-gather.18.cloned.1.call-done, bf16[1408,2048]{1,0:T(8,128)(2,1)} %all-gather.16.cloned.1.call-done), kind=kOutput, calls=%fused_computation.64 | convolution fusion | flops 5924323328 | bytes 27262976 | tf_op jit(solution)/shard_map/sd,fd->sf/dot_general | solution.py:148
  742.5 10.8 fusion.69
  753.3 20.0 %bitcast_add_fusion.2 = f32[1024,2048]{1,0:T(8,128)} fusion(f32[1024,2048,1]{1,0,2:T(8,128)} %fusion.69, bf16[2,2048,1408]{2,1,0:T(8,128)(2,1)} %all-gather.14.cloned.1.call-done, bf16[1,1024,1408]{2,1,0:T(8,128)(2,1)} %get-tuple-element.399, bf16[1,1024,1408]{2,1,0:T(8,128)(2,1)} %get-tuple-element.398), kind=kOutput, calls=%fused_computation.40 | convolution fusion | flops 11816140800 | bytes 34078720 | tf_op jit(solution)/shard_map/jsf,jdf->sd/dot_general | solution.py:199
  773.3 12.2 convolution_bitcast_fusion.2
  785.7 1.8 copy-done.30
  787.4 19.1 %convolution_bitcast_fusion = f32[2,2048,1408]{1,2,0:T(8,128)} fusion(bf16[1024,2048]{1,0:T(8,128)(2,1)} %all-gather.8.cloned.1.call-done, bf16[1,1024,1408]{2,1,0:T(8,128)(2,1)} %get-tuple-element.399, bf16[1,1024,1408]{2,1,0:T(8,128)(2,1)S(1)} %copy-done.30), kind=kOutput, calls=%fused_computation.39 | convolution fusion | flops 11814043648 | bytes 33030144 | tf_op jit(solution)/shard_map/sd,jsf->jdf/dot_general | solution.py:152
  807.8 6.5 fusion.75
  814.4 1.7 copy-done.13
  816.1 10.8 fusion.76
  827.6 1.7 copy.70
  829.3 87.1 %reduce-scatter.12.cloned.1.call-done = f32[256,2048]{1,0:T(8,128)} async-done(((f32[1024,2048]{1,0:T(8,128)}), f32[256,2048]{1,0:T(8,128)}) %reduce-scatter.12.cloned.1.call-update) | async-done | bytes 2097168 | tf_op jit(solution)/shard_map/reduce_scatter | solution.py:197
  916.4 4.2 fusion.50
  920.6 41.6 %all-reduce.4 = (f32[]{:T(128)}, f32[]{:T(128)}, f32[2048]{0:T(1024)S(1)}, f32[2048]{0:T(1024)S(1)}) all-reduce(f32[]{:T(128)} %get-tuple-element.353, f32[]{:T(128)} %fusion.68, f32[2048]{0:T(1024)S(1)} %get-tuple-element.349, f32[2048]{0:T(1024)S(1)} %get-tuple-element.352), channel_id=1, replica_groups=mesh['fsdp'=8,'tp'=4] {'fsdp','tp'}, use_global_device_ids=true, to_apply=%region_8.9 | all-reduce | flops 4098 | bytes 32784 | tf_op jit(solution)/shard_map/psum | solution.py:131
  964.7 5.0 fusion.49
  969.7 44.2 %reduce-scatter.14.cloned.1.call-done = f32[3,256,512]{1,2,0:T(8,128)} async-done(((f32[3,2048,512]{1,2,0:T(8,128)}), f32[3,256,512]{1,2,0:T(8,128)}) %reduce-scatter.14.cloned.1.call-update) | async-done | bytes 1572880 | tf_op jit(solution)/shard_map/reduce_scatter | solution.py:218
  1013.9 3.0 copy.64
  1016.9 147.0 %reduce-scatter.18.cloned.1.call-done = f32[2,256,1408]{1,2,0:T(8,128)} async-done(((f32[2,2048,1408]{1,2,0:T(8,128)}), f32[2,256,1408]{1,2,0:T(8,128)}) %reduce-scatter.18.cloned.1.call-update) | async-done | bytes 2883600 | tf_op jit(solution)/shard_map/reduce_scatter | solution.py:221
  1163.9 3.4 copy.65
  1167.3 52.1 %reduce-scatter.16.cloned.1.call-done = f32[512,256]{1,0:T(8,128)} async-done(((f32[512,2048]{1,0:T(8,128)}), f32[512,256]{1,0:T(8,128)}) %reduce-scatter.16.cloned.1.call-update) | async-done | bytes 524304 | tf_op jit(solution)/shard_map/reduce_scatter | solution.py:220
  1219.4 90.9 %reduce-scatter.20.cloned.1.call-done = f32[1408,256]{1,0:T(8,128)} async-done(((f32[1408,2048]{1,0:T(8,128)}), f32[1408,256]{1,0:T(8,128)}) %reduce-scatter.20.cloned.1.call-update) | async-done | bytes 1441808 | tf_op jit(solution)/shard_map/reduce_scatter | solution.py:222
  (165 shorter events, 31.5 us)
Async XLA Ops:
  7.2 49.8 %copy-start.14 = (bf16[3,256,512]{2,1,0:T(8,128)(2,1)S(1)}, bf16[3,256,512]{2,1,0:T(8,128)(2,1)}, u32[]{:S(2)}) copy-start(bf16[3,256,512]{2,1,0:T(8,128)(2,1)} %param.21) | copy-start | bytes 2359300
  7.2 130.6 %all-gather.8.cloned.1.call-start = ((), (), s32[]{:S(2)}) async-start(), calls=%async_computation.7 | async-start | bytes 5242880 | tf_op jit(solution)/shard_map/all_gather | solution.py:73
  8.8 49.4 %copy-start.23 = (f32[256]{0:T(256)}, f32[256]{0:T(256)S(1)}, u32[]{:S(2)}) copy-start(f32[256]{0:T(256)S(1)} %broadcast_multiply_fusion.3) | copy-start | bytes 3076
  10.4 48.5 %copy-start.25 = (f32[256]{0:T(256)}, f32[256]{0:T(256)S(1)}, u32[]{:S(2)}) copy-start(f32[256]{0:T(256)S(1)} %add_rsqrt_fusion) | copy-start | bytes 3076
  54.2 4.7 copy-start.21
  56.9 3.3 copy-start.29
  56.9 128.6 %all-gather.10.cloned.1.call-start = ((), (), s32[]{:S(2)}) async-start(), calls=%async_computation.8 | async-start | bytes 7077888 | tf_op jit(solution)/shard_map/all_gather | solution.py:58
  58.1 196.9 %all-gather.14.cloned.1.call-start = ((), (), s32[]{:S(2)}) async-start(), calls=%async_computation.10 | async-start | bytes 12976128 | tf_op jit(solution)/shard_map/all_gather | solution.py:61
  58.9 242.3 %all-gather.16.cloned.1.call-start = ((), (), s32[]{:S(2)}) async-start(), calls=%async_computation.11 | async-start | bytes 6488064 | tf_op jit(solution)/shard_map/all_gather | solution.py:62
  59.5 271.7 %all-gather.12.cloned.1.call-start = ((), (), s32[]{:S(2)}) async-start(), calls=%async_computation.9 | async-start | bytes 2359296 | tf_op jit(solution)/shard_map/all_gather | solution.py:60
  60.1 425.4 %reduce-scatter.10.cloned.1.call-start = ((), (), s32[]{:S(2)}) async-start(), calls=%async_computation.12 | async-start | bytes 10485760 | tf_op jit(solution)/shard_map/reduce_scatter | solution.py:120
  70.7 126.9 %copy-start.15 = (f32[1024,16]{0,1:T(8,128)}, f32[1024,16]{0,1:T(8,128)S(1)}, u32[]{:S(2)}) copy-start(f32[1024,16]{0,1:T(8,128)S(1)} %get-tuple-element.419) | copy-start | bytes 196612
  70.7 126.9 %copy-start.17 = (f32[1024,16]{0,1:T(8,128)}, f32[1024,16]{0,1:T(8,128)S(1)}, u32[]{:S(2)}) copy-start(f32[1024,16]{0,1:T(8,128)S(1)} %get-tuple-element.418) | copy-start | bytes 196612
  232.4 98.7 %copy-start.11 = (bf16[64,8,2,512]{3,1,2,0:T(8,128)(2,1)}, bf16[64,8,2,512]{3,1,2,0:T(8,128)(2,1)S(1)}, u32[]{:S(2)}) copy-start(bf16[64,8,2,512]{3,1,2,0:T(8,128)(2,1)S(1)} %copy.82) | copy-start | bytes 3145732
  272.3 4.2 copy-start.8
  340.9 144.7 %copy-start.4 = (bf16[256,2048]{1,0:T(8,128)(2,1)S(1)}, bf16[256,2048]{1,0:T(8,128)(2,1)}, u32[]{:S(2)}) copy-start(bf16[256,2048]{1,0:T(8,128)(2,1)} %param.15) | copy-start | bytes 3145732
  340.9 144.7 %copy-start.9 = (bf16[256,2048]{1,0:T(8,128)(2,1)S(1)}, bf16[256,2048]{1,0:T(8,128)(2,1)}, u32[]{:S(2)}) copy-start(bf16[256,2048]{1,0:T(8,128)(2,1)} %param.16) | copy-start | bytes 3145732
  340.9 230.0 %all-gather.18.cloned.1.call-start = ((), (), s32[]{:S(2)}) async-start(), calls=%async_computation.13 | async-start | bytes 5242880 | tf_op jit(solution)/shard_map/all_gather | solution.py:134
  341.7 147.4 %copy-start.27 = (f32[256]{0:T(256)}, f32[256]{0:T(256)S(1)}, u32[]{:S(2)}) copy-start(f32[256]{0:T(256)S(1)} %compare_convert_fusion) | copy-start | bytes 3076
  489.2 338.4 %reduce-scatter.22.cloned.1.call-start = ((), (), s32[]{:S(2)}) async-start(), calls=%async_computation.19 | async-start | bytes 294912
  577.4 3.8 copy-start.19
  598.4 9.4 copy-start.6
  607.8 8.9 copy-start
  616.7 2.7 copy-start.1
  622.3 21.7 %copy-start.2 = (f32[1024,8,64]{0,2,1:T(8,128)}, f32[1024,8,64]{0,2,1:T(8,128)S(1)}, u32[]{:S(2)}) copy-start(f32[1024,8,64]{0,2,1:T(8,128)S(1)} %bitcast_add_fusion.5) | copy-start | bytes 6291460 | tf_op jit(solution)/shard_map/while
  622.3 21.7 %copy-start.20 = (f32[2,8,512,1]{2,1,3,0:T(8,128)S(1)}, f32[2,8,512,1]{2,1,3,0:T(8,128)}, u32[]{:S(2)}) copy-start(f32[2,8,512,1]{2,1,3,0:T(8,128)} %copy-done.19) | copy-start | bytes 98308 | tf_op jit(solution)/shard_map/while
  644.0 3.8 copy-start.19
  665.0 9.4 copy-start.6
  674.4 9.6 copy-start
  683.9 2.7 copy-start.1
  689.5 21.7 %copy-start.2 = (f32[1024,8,64]{0,2,1:T(8,128)}, f32[1024,8,64]{0,2,1:T(8,128)S(1)}, u32[]{:S(2)}) copy-start(f32[1024,8,64]{0,2,1:T(8,128)S(1)} %bitcast_add_fusion.5) | copy-start | bytes 6291460 | tf_op jit(solution)/shard_map/while
  689.5 21.7 %copy-start.20 = (f32[2,8,512,1]{2,1,3,0:T(8,128)S(1)}, f32[2,8,512,1]{2,1,3,0:T(8,128)}, u32[]{:S(2)}) copy-start(f32[2,8,512,1]{2,1,3,0:T(8,128)} %copy-done.19) | copy-start | bytes 98308 | tf_op jit(solution)/shard_map/while
  711.4 6.0 copy-start.3
  711.4 6.9 copy-start.16
  715.6 2.7 copy-start.10
  717.3 1.2 copy-start.18
  726.8 189.6 %reduce-scatter.12.cloned.1.call-start = ((), (), s32[]{:S(2)}) async-start(), calls=%async_computation.14 | async-start | bytes 10485760 | tf_op jit(solution)/shard_map/reduce_scatter | solution.py:197
  773.3 240.6 %reduce-scatter.14.cloned.1.call-start = ((), (), s32[]{:S(2)}) async-start(), calls=%async_computation.15 | async-start | bytes 14155776 | tf_op jit(solution)/shard_map/reduce_scatter | solution.py:218
  785.6 1.8 copy-start.30
  785.6 378.3 %reduce-scatter.18.cloned.1.call-start = ((), (), s32[]{:S(2)}) async-start(), calls=%async_computation.17 | async-start | bytes 25952256 | tf_op jit(solution)/shard_map/reduce_scatter | solution.py:221
  806.6 1.3 copy-start.12
  806.6 412.8 %reduce-scatter.16.cloned.1.call-start = ((), (), s32[]{:S(2)}) async-start(), calls=%async_computation.16 | async-start | bytes 4718592 | tf_op jit(solution)/shard_map/reduce_scatter | solution.py:220
  814.3 1.8 copy-start.13
  814.3 496.0 %reduce-scatter.20.cloned.1.call-start = ((), (), s32[]{:S(2)}) async-start(), calls=%async_computation.18 | async-start | bytes 12976128 | tf_op jit(solution)/shard_map/reduce_scatter | solution.py:222
  826.9 89.5 %copy-start.5 = (bf16[256,2048]{1,0:T(8,128)(2,1)S(1)}, bf16[256,2048]{1,0:T(8,128)(2,1)}, u32[]{:S(2)}) copy-start(bf16[256,2048]{1,0:T(8,128)(2,1)} %param.15) | copy-start | bytes 3145732
  826.9 89.5 %copy-start.7 = (f32[256,2048]{1,0:T(8,128)S(1)}, f32[256,2048]{1,0:T(8,128)}, u32[]{:S(2)}) copy-start(f32[256,2048]{1,0:T(8,128)} %reduce-scatter.10.cloned.1.call-done) | copy-start | bytes 6291460
  826.9 89.5 %copy-start.22 = (f32[2048]{0:T(1024)S(1)}, f32[2048]{0:T(1024)}, u32[]{:S(2)}) copy-start(f32[2048]{0:T(1024)} %copy-done.21) | copy-start | bytes 24580
  826.9 89.5 %copy-start.24 = (f32[256]{0:T(256)S(1)}, f32[256]{0:T(256)}, u32[]{:S(2)}) copy-start(f32[256]{0:T(256)} %copy-done.23) | copy-start | bytes 3076
  826.9 89.5 %copy-start.26 = (f32[256]{0:T(256)S(1)}, f32[256]{0:T(256)}, u32[]{:S(2)}) copy-start(f32[256]{0:T(256)} %copy-done.25) | copy-start | bytes 3076
  826.9 89.5 %copy-start.28 = (f32[256]{0:T(256)S(1)}, f32[256]{0:T(256)}, u32[]{:S(2)}) copy-start(f32[256]{0:T(256)} %copy-done.27) | copy-start | bytes 3076
Sparse Core Ops, SparseCore 0:
  57.0 80.7 all-gather.7
  140.2 45.1 all-gather.9
  187.4 67.6 all-gather.13
  256.8 44.3 all-gather.15
  302.9 28.1 all-gather.11
  341.0 144.4 reduce-scatter.9
  489.3 81.4 all-gather.17
  726.9 32.1 reduce-scatter.21
  773.4 142.9 reduce-scatter.11
  920.1 93.7 reduce-scatter.13
  1018.0 145.9 reduce-scatter.17
  1168.1 51.2 reduce-scatter.15
  1223.5 86.7 reduce-scatter.19
where the time goes:
time: 1320 us
  waiting for transfers between devices  826 us (63%)
  matrix products  231 us (18%)
  blocking collectives  93.9 us (7%)
  local copies, waits for them, and re-layouts  81.9 us (6%)
  other arithmetic  59 us (4%)
  between operations  17.9 us (1%)
    reduce_scatter x1, waiting for transfers between devices, per_device(): lax.psum_scatter(grad_gu_w, 'fsdp', scatter_dimension=1, tiled=True)  147 us
    reduce_scatter x1, waiting for transfers between devices, per_device(): lax.psum_scatter(jnp.dot(attn_rows, w_out, preferred_element_type=jnp.flo...  144 us
    reduce_scatter x1, waiting for transfers between devices, per_device(): lax.psum_scatter(grad_down, 'fsdp', scatter_dimension=1, tiled=True)  90.9 us
    reduce_scatter x1, waiting for transfers between devices, per_device(): lax.psum_scatter(jnp.einsum('jse,jde->sd', grad_qkv, w_qkv, preferred_ele...  87.1 us
    all_gather x1, waiting for transfers between devices, per_device(): lax.all_gather(seed_rows.astype(jnp.bfloat16), 'tp', axis=0, tiled=True)  81.6 us
    all_gather x1, waiting for transfers between devices, per_device(): all_normed = lax.all_gather(normed, 'tp', axis=0, tiled=True)  67.1 us
    reduce_scatter x1, waiting for transfers between devices, per_device(): lax.psum_scatter(grad_out_w, 'fsdp', scatter_dimension=1, tiled=True)  52.1 us
    all_gather x1, waiting for transfers between devices, per_device(): lax.all_gather(qkv_weight, 'fsdp', axis=1, tiled=True)  47.7 us
  transfers between devices with their start and end apart: 13, of which 12 were waited for; matrix products, arithmetic and copies ran while one was open for 15% of the time, Pallas kernels for 0%

commit v1 on v0

--- a/solution.py
+++ b/solution.py
@@ -1,7 +1,9 @@
+import functools
 import jax
 import jax.numpy as jnp
 from jax import lax
 from jax.sharding import PartitionSpec as P
+from jax.lax import psum
 
 D = 2048
 HD = 64
@@ -9,6 +11,13 @@
 SEQ = 1024
 SEQS_DEV = 1
 epsilon = 1e-05
+
+
+def work_types_by_axis(s0, axis_name, comm_axis):
+    return psum(psum(s0, axis_name), comm_axis)
+
+
+see_units_now = functools.partial(work_types_by_axis, axis_name="fsdp", comm_axis="tp")
 
 
 def rotary_tables(row_total):
@@ -128,7 +137,7 @@
     mismatch = result - teacher.astype(jnp.float32)
     loss_part = jnp.sum(valid_rows[:, None] * mismatch * mismatch)
     count_part = jnp.sum(valid_rows)
-    loss_total, valid_total = lax.psum((loss_part, count_part), ("fsdp", "tp"))
+    loss_total, valid_total = see_units_now((loss_part, count_part))
     loss_value = loss_total / (valid_total * D)
     seed_rows = valid_rows[:, None] * (out_grad.astype(jnp.float32) + mismatch)
     all_seed = lax.all_gather(seed_rows.astype(jnp.bfloat16), "tp", axis=0, tiled=True)

time: 1320 us -> 1330 us (level)
  blocking collectives: 93.9 us -> 117 us
  waiting for transfers between devices: 826 us -> 804 us
    unnamed x1 -> x2, blocking collectives: 42 us -> 80.1 us
    reduce_scatter x1, waiting for transfers between devices: 44.2 us -> 21.9 us  [per_device(): lax.psum_scatter(grad_qkv_w, 'fsdp', scatter_dimension=1, tiled=True)]
    psum x1 -> x2, blocking collectives: 41.6 us -> 26.3 us  [work_types_by_axis(): return psum(psum(s0, axis_name), comm_axis)]
where the time goes in v1:
time: 1330 us; the launch traced here: 1320 us
  waiting for transfers between devices  804 us (60%)
  matrix products  231 us (17%)
  blocking collectives  117 us (9%)
  local copies, waits for them, and re-layouts  81.9 us (6%)
  other arithmetic  59.1 us (4%)
  between operations  17.9 us (1%)
    reduce_scatter x1, waiting for transfers between devices, per_device(): lax.psum_scatter(grad_gu_w, 'fsdp', scatter_dimension=1, tiled=True)  147 us
    reduce_scatter x1, waiting for transfers between devices, per_device(): lax.psum_scatter(jnp.dot(attn_rows, w_out, preferred_element_type=jnp.flo...  144 us
    reduce_scatter x1, waiting for transfers between devices, per_device(): lax.psum_scatter(grad_down, 'fsdp', scatter_dimension=1, tiled=True)  90.9 us
    reduce_scatter x1, waiting for transfers between devices, per_device(): lax.psum_scatter(jnp.einsum('jse,jde->sd', grad_qkv, w_qkv, preferred_ele...  87.1 us
    all_gather x1, waiting for transfers between devices, per_device(): lax.all_gather(seed_rows.astype(jnp.bfloat16), 'tp', axis=0, tiled=True)  81.6 us
    unnamed x2, blocking collectives  80.1 us
    all_gather x1, waiting for transfers between devices, per_device(): all_normed = lax.all_gather(normed, 'tp', axis=0, tiled=True)  67.1 us
    reduce_scatter x1, waiting for transfers between devices, per_device(): lax.psum_scatter(grad_out_w, 'fsdp', scatter_dimension=1, tiled=True)  52.1 us
  transfers between devices with their start and end apart: 13, of which 12 were waited for; matrix products, arithmetic and copies ran while one was open for 15% of the time, Pallas kernels for 0%

profile of v1, /device:TPU:0, one launch (start us, length us, event | category | flops | bytes accessed | tf_op | source)
XLA Modules:
  0.0 1318.6 jit_solution(9600857503685326756)
XLA Ops:
  12.2 42.0 %all-reduce.5 = (f32[2048]{0:T(1024)S(1)}, f32[2048]{0:T(1024)S(1)}) all-reduce(f32[2048]{0:T(1024)S(1)} %dynamic-update-slice.1, f32[2048]{0:T(1024)S(1)} %dynamic-update-slice), channel_id=1, replica_groups=mesh['fsdp'=8,'tp'=4] {'fsdp','tp'}, use_global_device_ids=true, to_apply=%add.1 | all-reduce | flops 4096 | bytes 32768
  54.2 2.7 fusion.44
  60.2 10.2 all-gather
  70.7 67.1 %all-gather.8.cloned.1.call-done = bf16[1024,2048]{1,0:T(8,128)(2,1)} async-done(((bf16[256,2048]{1,0:T(8,128)(2,1)}), bf16[1024,2048]{1,0:T(8,128)(2,1)}) %all-gather.8.cloned.1.call-update) | async-done | bytes 4194320 | tf_op jit(solution)/shard_map/all_gather | solution.py:82
  137.8 47.7 %all-gather.10.cloned.1.call-done = bf16[3,2048,512]{1,2,0:T(8,128)(2,1)} async-done(((bf16[3,256,512]{1,2,0:T(8,128)(2,1)}), bf16[3,2048,512]{1,2,0:T(8,128)(2,1)}) %all-gather.10.cloned.1.call-update) | async-done | bytes 6291472 | tf_op jit(solution)/shard_map/all_gather | solution.py:67
  185.5 10.1 add_bitcast_fusion
  199.0 32.1 %while.32 = (s32[]{:T(128)}, bf16[2,512,8,64]{1,3,2,0:T(8,128)(2,1)S(1)}, f32[2,8,512,1]{2,1,3,0:T(8,128)S(1)}, s32[2]{0:T(128)S(1)}, bf16[1024,8,64]{0,2,1:T(8,...) while((s32[]{:T(128)}, ...), condition=%wide.region_5.6_spmd.clone, body=%wide.region_2.5_spmd.clone.sunk | while | flops 1124594176 | bytes 56234364 | solution.py:124
  200.6 4.1 fusion.118
  204.8 4.2 fusion.119
  209.0 5.9 fusion.120
  216.6 4.1 fusion.118
  220.8 4.2 fusion.119
  225.0 5.9 fusion.120
  232.5 22.6 %all-gather.14.cloned.1.call-done = bf16[2,2048,1408]{2,1,0:T(8,128)(2,1)} async-done(((bf16[2,256,1408]{2,1,0:T(8,128)(2,1)}), bf16[2,2048,1408]{2,1,0:T(8,128)(2,1)}) %all-gather.14.cloned.1.call-update) | async-done | bytes 11534352 | tf_op jit(solution)/shard_map/all_gather | solution.py:70
  255.1 17.2 %convolution_bitcast_fusion.1 = f32[2,1024,1408]{2,1,0:T(8,128)S(1)} fusion(bf16[2,2048,1408]{2,1,0:T(8,128)(2,1)} %all-gather.14.cloned.1.call-done, bf16[1024,2048]{1,0:T(8,128)(2,1)} %all-gather.8.cloned.1.call-done), kind=kOutput, calls=%fused_computation.41 | convolution fusion | flops 11811160064 | bytes 27262976 | tf_op jit(solution)/shard_map/sd,jdf->jsf/dot_general | solution.py:126
  272.3 4.2 copy-done.8
  276.5 2.8 multiply_convert_fusion.3
  279.3 21.9 %all-gather.16.cloned.1.call-done = bf16[1408,2048]{1,0:T(8,128)(2,1)} async-done(((bf16[1408,256]{1,0:T(8,128)(2,1)}), bf16[1408,2048]{1,0:T(8,128)(2,1)}) %all-gather.16.cloned.1.call-update) | async-done | bytes 5767184 | tf_op jit(solution)/shard_map/all_gather | solution.py:71
  301.2 11.6 fusion.74
  312.9 18.3 %all-gather.12.cloned.1.call-done = bf16[512,2048]{1,0:T(8,128)(2,1)} async-done(((bf16[512,256]{1,0:T(8,128)(2,1)}), bf16[512,2048]{1,0:T(8,128)(2,1)}) %all-gather.12.cloned.1.call-update) | async-done | bytes 2097168 | tf_op jit(solution)/shard_map/all_gather | solution.py:69
  331.2 9.7 convolution_add_fusion
  341.7 143.8 %reduce-scatter.10.cloned.1.call-done = f32[256,2048]{1,0:T(8,128)} async-done(((f32[1024,2048]{1,0:T(8,128)}), f32[256,2048]{1,0:T(8,128)}) %reduce-scatter.10.cloned.1.call-update) | async-done | bytes 2097168 | tf_op jit(solution)/shard_map/reduce_scatter | solution.py:129
  485.5 3.7 fusion.59
  489.3 81.6 %all-gather.18.cloned.1.call-done = bf16[1024,2048]{1,0:T(8,128)(2,1)} async-done(((bf16[256,2048]{1,0:T(8,128)(2,1)}), bf16[1024,2048]{1,0:T(8,128)(2,1)}) %all-gather.18.cloned.1.call-update) | async-done | bytes 4194320 | tf_op jit(solution)/shard_map/all_gather | solution.py:143
  570.8 6.2 convolution_convert_fusion
  577.0 134.2 %while.33 = (s32[]{:T(128)}, f32[1024,8,64]{0,2,1:T(8,128)}, f32[1024,8,64]{0,2,1:T(8,128)}, f32[2,512,8,64]{1,0,3,2:T(2,128)}, s32[2]{0:T(128)S(1)}, /*index=5*...) while((s32[]{:T(128)}, f32[1024,8,64]{0,2,1:T(8,128)}, ...), condition=%wide.region_15.16_spmd.clone, body=%wide.region_13.15_spmd.clone.sunk | while | flops 2729701888 | bytes 200626816 | solution.py:189
  582.4 3.8 fusion.130
  586.2 12.2 multiply_reduce_fusion.3
  598.4 9.4 multiply_convert_fusion.5
  607.8 8.9 bitcast_add_fusion.6
  616.7 2.7 fusion.131
  619.3 2.9 bitcast_add_fusion.5
  622.2 2.1 copy.85
  624.3 19.7 %dynamic_update_slice.30 = f32[2,512,8,64]{1,0,3,2:T(2,128)} dynamic-update-slice(f32[2,512,8,64]{1,0,3,2:T(2,128)} %get-tuple-element.599, f32[1,512,8,64]{1,0,3,2:T(1,128)} %copy.85, s32[]{:T(128)S(6)} %copy.104, s32[]{:T(128)} %constant.200.clone.1..sunk.1, s32[]{:T(128)} %constant.200.clone.1..sunk.1, s32[]{:T(128)} %constant.200.clone.1..sunk.1) | dynamic-update-slice | bytes 2097156 | tf_op jit(solution)/shard_map/while/body/jit(dynamic_update_index_in_dim)/dynamic_update_slice | solution.py:124
  648.9 3.8 fusion.130
  652.7 12.2 multiply_reduce_fusion.3
  664.9 9.4 multiply_convert_fusion.5
  674.3 9.5 bitcast_add_fusion.6
  683.8 2.7 fusion.131
  686.5 2.9 bitcast_add_fusion.5
  689.4 2.1 copy.85
  691.4 19.7 %dynamic_update_slice.30 = f32[2,512,8,64]{1,0,3,2:T(2,128)} dynamic-update-slice(f32[2,512,8,64]{1,0,3,2:T(2,128)} %get-tuple-element.599, f32[1,512,8,64]{1,0,3,2:T(1,128)} %copy.85, s32[]{:T(128)S(6)} %copy.104, s32[]{:T(128)} %constant.200.clone.1..sunk.1, s32[]{:T(128)} %constant.200.clone.1..sunk.1, s32[]{:T(128)} %constant.200.clone.1..sunk.1) | dynamic-update-slice | bytes 2097156 | tf_op jit(solution)/shard_map/while/body/jit(dynamic_update_index_in_dim)/dynamic_update_slice | solution.py:124
  711.3 4.2 reshape.270
  721.0 2.7 convert.56
  726.7 15.7 %fusion.34 = (bf16[1,1024,1408]{2,1,0:T(8,128)(2,1)}, bf16[1,1024,1408]{2,1,0:T(8,128)(2,1)}) fusion(f32[2,1024,1408]{2,1,0:T(8,128)} %copy-done.8, bf16[1024,2048]{1,0:T(8,128)(2,1)} %all-gather.18.cloned.1.call-done, bf16[1408,2048]{1,0:T(8,128)(2,1)} %all-gather.16.cloned.1.call-done), kind=kOutput, calls=%fused_computation.64 | convolution fusion | flops 5924323328 | bytes 27262976 | tf_op jit(solution)/shard_map/sd,fd->sf/dot_general | solution.py:157
  742.4 10.8 fusion.69
  753.2 20.0 %bitcast_add_fusion.2 = f32[1024,2048]{1,0:T(8,128)} fusion(f32[1024,2048,1]{1,0,2:T(8,128)} %fusion.69, bf16[2,2048,1408]{2,1,0:T(8,128)(2,1)} %all-gather.14.cloned.1.call-done, bf16[1,1024,1408]{2,1,0:T(8,128)(2,1)} %get-tuple-element.401, bf16[1,1024,1408]{2,1,0:T(8,128)(2,1)} %get-tuple-element.400), kind=kOutput, calls=%fused_computation.40 | convolution fusion | flops 11816140800 | bytes 34078720 | tf_op jit(solution)/shard_map/jsf,jdf->sd/dot_general | solution.py:208
  773.3 12.2 convolution_bitcast_fusion.2
  785.6 1.8 copy-done.30
  787.3 19.1 %convolution_bitcast_fusion = f32[2,2048,1408]{1,2,0:T(8,128)} fusion(bf16[1024,2048]{1,0:T(8,128)(2,1)} %all-gather.8.cloned.1.call-done, bf16[1,1024,1408]{2,1,0:T(8,128)(2,1)} %get-tuple-element.401, bf16[1,1024,1408]{2,1,0:T(8,128)(2,1)S(1)} %copy-done.30), kind=kOutput, calls=%fused_computation.39 | convolution fusion | flops 11814043648 | bytes 33030144 | tf_op jit(solution)/shard_map/sd,jsf->jdf/dot_general | solution.py:161
  807.8 6.5 fusion.75
  816.1 10.8 fusion.76
  829.2 87.1 %reduce-scatter.12.cloned.1.call-done = f32[256,2048]{1,0:T(8,128)} async-done(((f32[1024,2048]{1,0:T(8,128)}), f32[256,2048]{1,0:T(8,128)}) %reduce-scatter.12.cloned.1.call-update) | async-done | bytes 2097168 | tf_op jit(solution)/shard_map/reduce_scatter | solution.py:206
  916.4 4.2 fusion.50
  920.5 14.1 %all-reduce.6 = (f32[]{:T(128)}, f32[]{:T(128)}) all-reduce(f32[]{:T(128)} %get-tuple-element.353, f32[]{:T(128)} %fusion.68), channel_id=1, replica_groups=mesh['fsdp'=8,'tp'=4] {'fsdp'}, use_global_device_ids=true, to_apply=%region_8.9 | all-reduce | flops 2 | bytes 16 | tf_op jit(solution)/shard_map/psum | solution.py:17
  934.6 12.2 all-reduce.7
  946.8 38.0 %all-reduce.4 = (f32[2048]{0:T(1024)S(1)}, f32[2048]{0:T(1024)S(1)}) all-reduce(f32[2048]{0:T(1024)S(1)} %get-tuple-element.349, f32[2048]{0:T(1024)S(1)} %get-tuple-element.352), channel_id=4, replica_groups=mesh['fsdp'=8,'tp'=4] {'fsdp','tp'}, use_global_device_ids=true, to_apply=%region_20.21.clone | all-reduce | flops 4096 | bytes 32768
  987.3 5.1 fusion.49
  992.4 21.9 %reduce-scatter.14.cloned.1.call-done = f32[3,256,512]{1,2,0:T(8,128)} async-done(((f32[3,2048,512]{1,2,0:T(8,128)}), f32[3,256,512]{1,2,0:T(8,128)}) %reduce-scatter.14.cloned.1.call-update) | async-done | bytes 1572880 | tf_op jit(solution)/shard_map/reduce_scatter | solution.py:227
  1014.3 3.0 copy.64
  1017.3 147.0 %reduce-scatter.18.cloned.1.call-done = f32[2,256,1408]{1,2,0:T(8,128)} async-done(((f32[2,2048,1408]{1,2,0:T(8,128)}), f32[2,256,1408]{1,2,0:T(8,128)}) %reduce-scatter.18.cloned.1.call-update) | async-done | bytes 2883600 | tf_op jit(solution)/shard_map/reduce_scatter | solution.py:230
  1164.3 3.4 copy.65
  1167.7 52.1 %reduce-scatter.16.cloned.1.call-done = f32[512,256]{1,0:T(8,128)} async-done(((f32[512,2048]{1,0:T(8,128)}), f32[512,256]{1,0:T(8,128)}) %reduce-scatter.16.cloned.1.call-update) | async-done | bytes 524304 | tf_op jit(solution)/shard_map/reduce_scatter | solution.py:229
  1219.8 90.9 %reduce-scatter.20.cloned.1.call-done = f32[1408,256]{1,0:T(8,128)} async-done(((f32[1408,2048]{1,0:T(8,128)}), f32[1408,256]{1,0:T(8,128)}) %reduce-scatter.20.cloned.1.call-update) | async-done | bytes 1441808 | tf_op jit(solution)/shard_map/reduce_scatter | solution.py:231
  (167 shorter events, 34.9 us)
Async XLA Ops:
  7.2 49.8 %copy-start.14 = (bf16[3,256,512]{2,1,0:T(8,128)(2,1)S(1)}, bf16[3,256,512]{2,1,0:T(8,128)(2,1)}, u32[]{:S(2)}) copy-start(bf16[3,256,512]{2,1,0:T(8,128)(2,1)} %param.21) | copy-start | bytes 2359300
  7.2 130.6 %all-gather.8.cloned.1.call-start = ((), (), s32[]{:S(2)}) async-start(), calls=%async_computation.7 | async-start | bytes 5242880 | tf_op jit(solution)/shard_map/all_gather | solution.py:82
  8.8 49.4 %copy-start.23 = (f32[256]{0:T(256)}, f32[256]{0:T(256)S(1)}, u32[]{:S(2)}) copy-start(f32[256]{0:T(256)S(1)} %broadcast_multiply_fusion.3) | copy-start | bytes 3076
  10.4 48.5 %copy-start.25 = (f32[256]{0:T(256)}, f32[256]{0:T(256)S(1)}, u32[]{:S(2)}) copy-start(f32[256]{0:T(256)S(1)} %add_rsqrt_fusion) | copy-start | bytes 3076
  54.2 4.7 copy-start.21
  56.9 3.3 copy-start.29
  56.9 128.6 %all-gather.10.cloned.1.call-start = ((), (), s32[]{:S(2)}) async-start(), calls=%async_computation.8 | async-start | bytes 7077888 | tf_op jit(solution)/shard_map/all_gather | solution.py:67
  58.2 196.9 %all-gather.14.cloned.1.call-start = ((), (), s32[]{:S(2)}) async-start(), calls=%async_computation.10 | async-start | bytes 12976128 | tf_op jit(solution)/shard_map/all_gather | solution.py:70
  58.9 242.3 %all-gather.16.cloned.1.call-start = ((), (), s32[]{:S(2)}) async-start(), calls=%async_computation.11 | async-start | bytes 6488064 | tf_op jit(solution)/shard_map/all_gather | solution.py:71
  59.5 271.7 %all-gather.12.cloned.1.call-start = ((), (), s32[]{:S(2)}) async-start(), calls=%async_computation.9 | async-start | bytes 2359296 | tf_op jit(solution)/shard_map/all_gather | solution.py:69
  60.1 425.4 %reduce-scatter.10.cloned.1.call-start = ((), (), s32[]{:S(2)}) async-start(), calls=%async_computation.12 | async-start | bytes 10485760 | tf_op jit(solution)/shard_map/reduce_scatter | solution.py:129
  70.7 126.9 %copy-start.15 = (f32[1024,16]{0,1:T(8,128)}, f32[1024,16]{0,1:T(8,128)S(1)}, u32[]{:S(2)}) copy-start(f32[1024,16]{0,1:T(8,128)S(1)} %get-tuple-element.421) | copy-start | bytes 196612
  70.7 126.9 %copy-start.17 = (f32[1024,16]{0,1:T(8,128)}, f32[1024,16]{0,1:T(8,128)S(1)}, u32[]{:S(2)}) copy-start(f32[1024,16]{0,1:T(8,128)S(1)} %get-tuple-element.420) | copy-start | bytes 196612
  232.5 98.7 %copy-start.11 = (bf16[64,8,2,512]{3,1,2,0:T(8,128)(2,1)}, bf16[64,8,2,512]{3,1,2,0:T(8,128)(2,1)S(1)}, u32[]{:S(2)}) copy-start(bf16[64,8,2,512]{3,1,2,0:T(8,128)(2,1)S(1)} %copy.82) | copy-start | bytes 3145732
  272.3 4.2 copy-start.8
  340.8 144.7 %copy-start.4 = (bf16[256,2048]{1,0:T(8,128)(2,1)S(1)}, bf16[256,2048]{1,0:T(8,128)(2,1)}, u32[]{:S(2)}) copy-start(bf16[256,2048]{1,0:T(8,128)(2,1)} %param.15) | copy-start | bytes 3145732
  340.8 144.7 %copy-start.9 = (bf16[256,2048]{1,0:T(8,128)(2,1)S(1)}, bf16[256,2048]{1,0:T(8,128)(2,1)}, u32[]{:S(2)}) copy-start(bf16[256,2048]{1,0:T(8,128)(2,1)} %param.16) | copy-start | bytes 3145732
  340.9 230.0 %all-gather.18.cloned.1.call-start = ((), (), s32[]{:S(2)}) async-start(), calls=%async_computation.13 | async-start | bytes 5242880 | tf_op jit(solution)/shard_map/all_gather | solution.py:143
  341.7 147.4 %copy-start.27 = (f32[256]{0:T(256)}, f32[256]{0:T(256)S(1)}, u32[]{:S(2)}) copy-start(f32[256]{0:T(256)S(1)} %compare_convert_fusion) | copy-start | bytes 3076
  489.2 338.3 %reduce-scatter.22.cloned.1.call-start = ((), (), s32[]{:S(2)}) async-start(), calls=%async_computation.19 | async-start | bytes 294912
  577.4 3.8 copy-start.19
  598.4 9.4 copy-start.6
  607.8 8.9 copy-start
  616.7 2.7 copy-start.1
  622.2 21.7 %copy-start.2 = (f32[1024,8,64]{0,2,1:T(8,128)}, f32[1024,8,64]{0,2,1:T(8,128)S(1)}, u32[]{:S(2)}) copy-start(f32[1024,8,64]{0,2,1:T(8,128)S(1)} %bitcast_add_fusion.5) | copy-start | bytes 6291460 | tf_op jit(solution)/shard_map/while
  622.2 21.7 %copy-start.20 = (f32[2,8,512,1]{2,1,3,0:T(8,128)S(1)}, f32[2,8,512,1]{2,1,3,0:T(8,128)}, u32[]{:S(2)}) copy-start(f32[2,8,512,1]{2,1,3,0:T(8,128)} %copy-done.19) | copy-start | bytes 98308 | tf_op jit(solution)/shard_map/while
  643.9 3.8 copy-start.19
  664.9 9.4 copy-start.6
  674.3 9.6 copy-start
  683.8 2.7 copy-start.1
  689.3 21.7 %copy-start.2 = (f32[1024,8,64]{0,2,1:T(8,128)}, f32[1024,8,64]{0,2,1:T(8,128)S(1)}, u32[]{:S(2)}) copy-start(f32[1024,8,64]{0,2,1:T(8,128)S(1)} %bitcast_add_fusion.5) | copy-start | bytes 6291460 | tf_op jit(solution)/shard_map/while
  689.4 21.7 %copy-start.20 = (f32[2,8,512,1]{2,1,3,0:T(8,128)S(1)}, f32[2,8,512,1]{2,1,3,0:T(8,128)}, u32[]{:S(2)}) copy-start(f32[2,8,512,1]{2,1,3,0:T(8,128)} %copy-done.19) | copy-start | bytes 98308 | tf_op jit(solution)/shard_map/while
  711.3 5.9 copy-start.3
  711.3 6.9 copy-start.16
  715.5 2.7 copy-start.10
  717.2 1.2 copy-start.18
  726.6 189.7 %reduce-scatter.12.cloned.1.call-start = ((), (), s32[]{:S(2)}) async-start(), calls=%async_computation.14 | async-start | bytes 10485760 | tf_op jit(solution)/shard_map/reduce_scatter | solution.py:206
  773.2 241.1 %reduce-scatter.14.cloned.1.call-start = ((), (), s32[]{:S(2)}) async-start(), calls=%async_computation.15 | async-start | bytes 14155776 | tf_op jit(solution)/shard_map/reduce_scatter | solution.py:227
  785.5 1.8 copy-start.30
  785.5 378.8 %reduce-scatter.18.cloned.1.call-start = ((), (), s32[]{:S(2)}) async-start(), calls=%async_computation.17 | async-start | bytes 25952256 | tf_op jit(solution)/shard_map/reduce_scatter | solution.py:230
  806.5 1.3 copy-start.12
  806.5 413.3 %reduce-scatter.16.cloned.1.call-start = ((), (), s32[]{:S(2)}) async-start(), calls=%async_computation.16 | async-start | bytes 4718592 | tf_op jit(solution)/shard_map/reduce_scatter | solution.py:229
  814.2 1.8 copy-start.13
  814.3 496.4 %reduce-scatter.20.cloned.1.call-start = ((), (), s32[]{:S(2)}) async-start(), calls=%async_computation.18 | async-start | bytes 12976128 | tf_op jit(solution)/shard_map/reduce_scatter | solution.py:231
  826.8 89.5 %copy-start.5 = (bf16[256,2048]{1,0:T(8,128)(2,1)S(1)}, bf16[256,2048]{1,0:T(8,128)(2,1)}, u32[]{:S(2)}) copy-start(bf16[256,2048]{1,0:T(8,128)(2,1)} %param.15) | copy-start | bytes 3145732
  826.8 89.5 %copy-start.7 = (f32[256,2048]{1,0:T(8,128)S(1)}, f32[256,2048]{1,0:T(8,128)}, u32[]{:S(2)}) copy-start(f32[256,2048]{1,0:T(8,128)} %reduce-scatter.10.cloned.1.call-done) | copy-start | bytes 6291460
  826.8 89.5 %copy-start.22 = (f32[2048]{0:T(1024)S(1)}, f32[2048]{0:T(1024)}, u32[]{:S(2)}) copy-start(f32[2048]{0:T(1024)} %copy-done.21) | copy-start | bytes 24580
  826.8 89.5 %copy-start.24 = (f32[256]{0:T(256)S(1)}, f32[256]{0:T(256)}, u32[]{:S(2)}) copy-start(f32[256]{0:T(256)} %copy-done.23) | copy-start | bytes 3076
  826.8 89.5 %copy-start.26 = (f32[256]{0:T(256)S(1)}, f32[256]{0:T(256)}, u32[]{:S(2)}) copy-start(f32[256]{0:T(256)} %copy-done.25) | copy-start | bytes 3076
  826.8 89.5 %copy-start.28 = (f32[256]{0:T(256)S(1)}, f32[256]{0:T(256)}, u32[]{:S(2)}) copy-start(f32[256]{0:T(256)} %copy-done.27) | copy-start | bytes 3076
Sparse Core Ops, SparseCore 0:
  57.0 80.7 all-gather.7
  140.2 45.1 all-gather.9
  187.4 67.6 all-gather.13
  256.8 44.3 all-gather.15
  302.9 28.1 all-gather.11
  341.0 144.4 reduce-scatter.9
  489.3 81.4 all-gather.17
  726.7 32.1 reduce-scatter.21
  773.3 142.9 reduce-scatter.11
  920.1 94.1 reduce-scatter.13
  1018.3 145.9 reduce-scatter.17
  1168.4 51.2 reduce-scatter.15
  1223.9 86.7 reduce-scatter.19
